TPU v7x, 32 devices: a whole 2x2x4 slice. The times are simulated.
32 devices in a mesh: pair: 8 (over z, x), col: 4 (over y, core).
Axes of the slice: x: 2, y: 2, z: 4, core: 2. Of those that a mesh axis runs over, the one named last changes fastest.
Arguments:
- point_values: bfloat16 [32768, 1024], P('pair', 'col'), may hold values from -2 to 2, as said below
- grid_values: bfloat16 [32768, 512], P('pair'), may hold values from -6 to 6
Outputs:
- fitted: float32 [512, 1024], P(('pair', 'col'))
Inputs may be any that keep to these rules, and one draw needn't show every extreme that they name: `point_values`: real pair-product values.
All inputs are finite; a program needn't handle non-finite values.
Results may differ from a plain program's by a relative error of at most 0.0003.
Values may be sent and summed in bfloat16 or wider, within the bound.
A program may use at most 128 MiB of HBM per device.

v0:
```python
import jax
import jax.numpy as jnp
from jax import lax
from jax.sharding import PartitionSpec as P


def cross(left, right):
    return lax.dot_general(
        left, right, (((0,), (0,)), ((), ())), preferred_element_type=jnp.float32
    )


def body(point_values, grid_values):
    gathered = lax.all_gather(point_values, "col", axis=1, tiled=True)
    gram = lax.psum(cross(gathered, gathered), "pair")
    factor = jnp.linalg.cholesky(gram)
    summed = lax.psum_scatter(
        cross(grid_values, point_values), "pair", scatter_dimension=0, tiled=True
    )
    regrouped = lax.all_to_all(summed, "col", split_axis=0, concat_axis=1, tiled=True)
    solved = jax.scipy.linalg.cho_solve((factor, True), regrouped.T)
    return solved.T


def solution(mesh):
    in_specs = (P("pair", "col"), P("pair", None))
    out_specs = P(("pair", "col"), None)
    return jax.shard_map(body, mesh=mesh, in_specs=in_specs, out_specs=out_specs, check_vma=False)
```

profile of v0, /device:TPU:0, one launch (start us, length us, event | category | flops | bytes accessed | tf_op | source)
XLA Modules:
  0.0 594.1 jit_solution(14145770324071007327)
XLA Ops:
  8.1 5.0 fusion.96
  13.2 58.8 %all-gather.2.cloned.1.call-done = bf16[4096,1024]{1,0:T(8,128)(2,1)} async-done(((bf16[4096,256]{1,0:T(8,128)(2,1)}), bf16[4096,1024]{1,0:T(8,128)(2,1)}) %all-gather.2.cloned.1.call-update) | async-done | bytes 8388624 | tf_op jit(solution)/shard_map/all_gather | solution.py:14
  72.0 15.1 %fusion.95 = f32[1024,1024]{0,1:T(8,128)} fusion(bf16[4096,1024]{1,0:T(8,128)(2,1)} %all-gather.2.cloned.1.call-done), kind=kOutput, calls=%fused_computation.213 | convolution fusion | flops 8589934592 | bytes 12582912 | tf_op jit(solution)/shard_map/dot_general | solution.py:8
  94.5 148.8 %all-reduce.3.cloned.1.call-done = f32[1024,1024]{0,1:T(8,128)} async-done(((f32[1024,1024]{0,1:T(8,128)}), f32[1024,1024]{0,1:T(8,128)}) %all-reduce.3.cloned.1.call-update) | async-done | bytes 4194320 | tf_op jit(solution)/shard_map/psum | solution.py:15
  243.3 5.6 copy.9
  248.9 4.4 fusion
  255.3 11.7 %cholesky.223 = f32[128,128]{1,0:T(8,128)S(1)} custom-call(f32[128,128]{1,0:T(8,128)S(1)} %cholesky.580), custom_call_target="Cholesky" | custom-call | tf_op jit(solution)/shard_map/jit(cholesky)/cholesky | solution.py:16
  267.0 9.8 %custom-call.66 = f32[1,128,128]{1,2,0:T(8,128)S(1)} custom-call(f32[1,128,128]{2,1,0:T(8,128)S(1)} %get-tuple-element.44), custom_call_target="InvertDiagBlocksLowerTriangular" | custom-call | tf_op jit(solution)/shard_map/jit(cholesky)/cholesky | solution.py:16
  283.3 12.2 %cholesky.244 = f32[128,128]{1,0:T(8,128)S(1)} custom-call(f32[128,128]{1,0:T(8,128)S(1)} %cholesky.584), custom_call_target="Cholesky" | custom-call | tf_op jit(solution)/shard_map/jit(cholesky)/cholesky | solution.py:16
  296.2 9.8 %custom-call.67 = f32[1,128,128]{1,2,0:T(8,128)S(1)} custom-call(f32[1,128,128]{2,1,0:T(8,128)S(1)} %get-tuple-element.41), custom_call_target="InvertDiagBlocksLowerTriangular" | custom-call | tf_op jit(solution)/shard_map/jit(cholesky)/cholesky | solution.py:16
  309.3 11.7 %cholesky.468 = f32[128,128]{1,0:T(8,128)S(1)} custom-call(f32[128,128]{1,0:T(8,128)S(1)} %cholesky.589), custom_call_target="Cholesky" | custom-call | tf_op jit(solution)/shard_map/jit(cholesky)/cholesky | solution.py:16
  322.3 9.8 %custom-call.68 = f32[1,128,128]{1,2,0:T(8,128)S(1)} custom-call(f32[1,128,128]{2,1,0:T(8,128)S(1)} %get-tuple-element.38), custom_call_target="InvertDiagBlocksLowerTriangular" | custom-call | tf_op jit(solution)/shard_map/jit(cholesky)/cholesky | solution.py:16
  335.6 11.8 %cholesky.487 = f32[128,128]{1,0:T(8,128)S(1)} custom-call(f32[128,128]{1,0:T(8,128)S(1)} %cholesky.594), custom_call_target="Cholesky" | custom-call | tf_op jit(solution)/shard_map/jit(cholesky)/cholesky | solution.py:16
  348.8 9.8 %custom-call.69 = f32[1,128,128]{1,2,0:T(8,128)S(1)} custom-call(f32[1,128,128]{2,1,0:T(8,128)S(1)} %get-tuple-element.35), custom_call_target="InvertDiagBlocksLowerTriangular" | custom-call | tf_op jit(solution)/shard_map/jit(cholesky)/cholesky | solution.py:16
  362.0 11.7 %cholesky.506 = f32[128,128]{1,0:T(8,128)S(1)} custom-call(f32[128,128]{1,0:T(8,128)S(1)} %cholesky.599), custom_call_target="Cholesky" | custom-call | tf_op jit(solution)/shard_map/jit(cholesky)/cholesky | solution.py:16
  375.0 10.0 %custom-call.70 = f32[1,128,128]{1,2,0:T(8,128)S(1)} custom-call(f32[1,128,128]{2,1,0:T(8,128)S(1)} %get-tuple-element.32), custom_call_target="InvertDiagBlocksLowerTriangular" | custom-call | tf_op jit(solution)/shard_map/jit(cholesky)/cholesky | solution.py:16
  388.3 11.7 %cholesky.526 = f32[128,128]{1,0:T(8,128)S(1)} custom-call(f32[128,128]{1,0:T(8,128)S(1)} %cholesky.604), custom_call_target="Cholesky" | custom-call | tf_op jit(solution)/shard_map/jit(cholesky)/cholesky | solution.py:16
  401.3 9.8 %custom-call.71 = f32[1,128,128]{1,2,0:T(8,128)S(1)} custom-call(f32[1,128,128]{2,1,0:T(8,128)S(1)} %get-tuple-element.29), custom_call_target="InvertDiagBlocksLowerTriangular" | custom-call | tf_op jit(solution)/shard_map/jit(cholesky)/cholesky | solution.py:16
  414.1 12.1 %cholesky.546 = f32[128,128]{1,0:T(8,128)S(1)} custom-call(f32[128,128]{1,0:T(8,128)S(1)} %cholesky.609), custom_call_target="Cholesky" | custom-call | tf_op jit(solution)/shard_map/jit(cholesky)/cholesky | solution.py:16
  427.5 9.8 %custom-call.72 = f32[1,128,128]{1,2,0:T(8,128)S(1)} custom-call(f32[1,128,128]{2,1,0:T(8,128)S(1)} %get-tuple-element.26), custom_call_target="InvertDiagBlocksLowerTriangular" | custom-call | tf_op jit(solution)/shard_map/jit(cholesky)/cholesky | solution.py:16
  439.9 11.7 %cholesky.564 = f32[128,128]{1,0:T(8,128)S(1)} custom-call(f32[128,128]{1,0:T(8,128)S(1)} %convolution_subtract_fusion.6), custom_call_target="Cholesky" | custom-call | tf_op jit(solution)/shard_map/jit(cholesky)/cholesky | solution.py:16
  458.5 4.8 select_select_fusion
  463.2 22.8 %while.1 = (s32[]{:T(128)}, f32[1024,1024]{1,0:T(8,128)}, s32[8,2]{0,1:T(2,128)S(1)}, f32[8,128,128]{2,1,0:T(8,128)S(1)}, s32[]{:T(128)}) while((s32[]{:T(128)}, f32[1024,1024]{1,0:T(8,128)}, s32[8,2]{0,1:T(2,128)S(1)}, f32[8,128,128]{2,1,0:T(8,128)S(1)}, s32[]{:T(128)}) %tuple.56), condition=%wide.while_cond, body=%wide.while_body.sunk | while | flops 2 | bytes 131181 | solution.py:21
  486.1 78.8 %custom-call.73 = f32[8,128,128]{1,2,0:T(8,128)S(1)} custom-call(f32[8,128,128]{2,1,0:T(8,128)S(1)} %get-tuple-element.12), custom_call_target="InvertDiagBlocksLowerTriangular" | custom-call | tf_op jit(solution)/shard_map/jit(_cho_solve)/triangular_solve | solution.py:21
  (130 shorter events, 88.9 us)
Async XLA Ops:
  7.4 64.6 %all-gather.2.cloned.1.call-start = ((), (), s32[]{:S(2)}) async-start(), calls=%async_computation.2 | async-start | bytes 10485760 | tf_op jit(solution)/shard_map/all_gather | solution.py:14
  8.1 79.0 %reduce-scatter.2.cloned.1.call-start = ((), (), s32[]{:S(2)}) async-start(), calls=%async_computation.4 | async-start | bytes 589824 | tf_op jit(solution)/shard_map/reduce_scatter | solution.py:17
  13.1 230.2 %all-reduce.3.cloned.1.call-start = ((), (), s32[]{:S(2)}) async-start(), calls=%async_computation.3 | async-start | bytes 8388608 | tf_op jit(solution)/shard_map/psum | solution.py:15
  87.1 7.4 %all-to-all-start = ((f32[4,16,256]{2,1,0:T(8,128)}), f32[4,16,256]{2,1,0:T(8,128)S(1)}, u32[]{:S(2)}, u32[]{:S(2)}) async-start(f32[4,16,256]{2,1,0:T(8,128)} %bitcast.147), calls=%async_computation.1 | async-start | bytes 131072 | tf_op jit(solution)/shard_map/all_to_all | solution.py:20
  253.4 1.9 copy-start
  585.8 0.6 copy-start.1
Sparse Core Ops, SparseCore 0:
  9.8 62.1 all-gather.1
Sparse Core Ops, SparseCore 1:
  13.2 64.7 reduce-scatter.1
  87.2 156.1 all-reduce.2
where the time goes:
time: 600 us; the launch traced here: 594 us
  other arithmetic  261 us (44%)
  waiting for transfers between devices  212 us (35%)
  matrix products  63.6 us (11%)
  local copies, waits for them, and re-layouts  33.6 us (6%)
  between operations  20.3 us (3%)
    another operation x30, other arithmetic, body(): factor = jnp.linalg.cholesky(gram)  173 us
    psum x1, waiting for transfers between devices, body(): gram = lax.psum(cross(gathered, gathered), 'pair')  149 us
    another operation x3, other arithmetic, body(): solved = jax.scipy.linalg.cho_solve((factor, True), regrouped.T)  83.6 us
    all_gather x1, waiting for transfers between devices, body(): gathered = lax.all_gather(point_values, 'col', axis=1, tiled=True)  58.8 us
    another operation x14, matrix products, body(): factor = jnp.linalg.cholesky(gram)  23.1 us
    another operation x24, local copies, waits for them, and re-layouts  22.7 us
    another operation x30, matrix products, body(): solved = jax.scipy.linalg.cho_solve((factor, True), regrouped.T)  20.5 us
    dot_general x2, matrix products, cross(): lax.dot_general(left, right, (((0,), (0,)), ((), ())), preferred_element_...  20 us
  transfers between devices with their start and end apart: 4, of which 3 were waited for; matrix products, arithmetic and copies ran while one was open for 3% of the time, Pallas kernels for 0%

commit v1 on v0

v1 whole, which is shorter than its diff:
```python
import functools

import jax
import jax.numpy as jnp
from jax import lax
from jax.experimental import pallas as pl
from jax.experimental.pallas import tpu as pltpu
from jax.sharding import PartitionSpec as P

NB = 128
TILE = 8
PANEL = 8


def cross(left, right):
    return lax.dot_general(
        left, right, (((0,), (0,)), ((), ())), preferred_element_type=jnp.float32
    )


def dot(left, right):
    return lax.dot_general(
        left, right, (((1,), (0,)), ((), ())),
        precision=lax.Precision.HIGHEST, preferred_element_type=jnp.float32,
    )


def invert(tiles):
    count = len(tiles)
    lane = lax.broadcasted_iota(jnp.int32, (TILE, NB), 1)
    sub = lax.broadcasted_iota(jnp.int32, (TILE, NB), 0)
    for start in range(0, NB, PANEL):
        cols = [
            [jnp.broadcast_to(t[:, start + k : start + k + 1], (TILE, NB)) for t in tiles]
            for k in range(PANEL)
        ]
        for k in range(PANEL):
            j = start + k
            at, s = divmod(j, TILE)
            here, on_row = lane == j, sub == s
            inv = 1.0 / jnp.broadcast_to(cols[k][at][s : s + 1, :], (TILE, NB))
            row = jnp.broadcast_to(tiles[at][s : s + 1, :], (TILE, NB)) * inv
            row = jnp.where(here, inv, row)
            c = list(cols[k])
            c[at] = jnp.where(on_row, -1.0, c[at])
            for m in range(k + 1, PANEL):
                r = jnp.broadcast_to(cols[m][at][s : s + 1, :], (TILE, NB)) * inv
                old = list(cols[m])
                old[at] = jnp.where(on_row, 0.0, old[at])
                cols[m] = [old[i] - c[i] * r for i in range(count)]
            old = [jnp.where(here, 0.0, t) for t in tiles]
            old[at] = jnp.where(on_row, 0.0, old[at])
            tiles = [old[i] - c[i] * row for i in range(count)]
    return tiles


def solve_kernel(cols, gram_ref, rhs_ref, out_ref, work, inverse):
    n = work.shape[1]
    rows = rhs_ref.shape[0]
    blocks = n // NB
    width = n // cols
    for i in range(gram_ref.shape[0]):
        p, c = divmod(i, cols)
        height = gram_ref.shape[1]
        work[p * height : (p + 1) * height, c * width : (c + 1) * width] = gram_ref[i]
    work[n : n + rows, :] = rhs_ref[...]

    def step(k, carry):
        for kk in range(blocks):
            @pl.when(k == kk)
            def _():
                inverse[...] = work[kk * NB : (kk + 1) * NB, kk * NB : (kk + 1) * NB]

        tiles = invert([inverse[i : i + TILE, :] for i in range(0, NB, TILE)])
        for i, t in enumerate(tiles):
            inverse[i * TILE : (i + 1) * TILE, :] = t

        for kk in range(blocks):
            @pl.when(k == kk)
            def _():
                lo, hi = kk * NB, (kk + 1) * NB
                scaled = dot(work[hi : n + rows, lo:hi], inverse[...])
                work[hi : n + rows, lo:hi] = scaled
                if hi < n:
                    work[hi : n + rows, hi:n] -= dot(scaled, work[lo:hi, hi:n])
        return carry

    lax.fori_loop(0, blocks, step, 0)
    for kk in range(blocks - 1, -1, -1):
        lo, hi = kk * NB, (kk + 1) * NB
        x = work[n : n + rows, lo:hi]
        if hi < n:
            x = x - dot(out_ref[:, hi:n], work[hi:n, lo:hi])
        out_ref[:, lo:hi] = x


def solve(gram_parts, rhs, cols):
    rows, n = rhs.shape
    vmem = pl.BlockSpec(memory_space=pltpu.VMEM)
    return pl.pallas_call(
        functools.partial(solve_kernel, cols),
        out_shape=jax.ShapeDtypeStruct((rows, n), jnp.float32),
        in_specs=[vmem, vmem],
        out_specs=vmem,
        scratch_shapes=[
            pltpu.VMEM((n + rows, n), jnp.float32),
            pltpu.VMEM((NB, NB), jnp.float32),
        ],
        compiler_params=pltpu.CompilerParams(vmem_limit_bytes=48 << 20),
    )(gram_parts, rhs)


def solution(mesh):
    cols = mesh.shape["col"]

    def body(point_values, grid_values):
        gathered = lax.all_gather(point_values, "col", axis=1, tiled=True)
        gram = lax.psum_scatter(
            cross(gathered, point_values), "pair", scatter_dimension=0, tiled=True
        )
        gram_parts = lax.all_gather(gram, ("pair", "col"), axis=0, tiled=False)
        summed = lax.psum_scatter(
            cross(grid_values, point_values), "pair", scatter_dimension=0, tiled=True
        )
        regrouped = lax.all_to_all(summed, "col", split_axis=0, concat_axis=1, tiled=True)
        return solve(gram_parts, regrouped, cols)

    in_specs = (P("pair", "col"), P("pair", None))
    out_specs = P(("pair", "col"), None)
    return jax.shard_map(body, mesh=mesh, in_specs=in_specs, out_specs=out_specs, check_vma=False)
```

time: 600 us -> 349 us (0.58)
  other arithmetic: 261 us -> 0 us
  Pallas kernels: 0 us -> 69.3 us
  matrix products: 63.6 us -> 11.7 us
  waiting for transfers between devices: 212 us -> 245 us
  local copies, waits for them, and re-layouts: 33.6 us -> 2.2 us
  blocking collectives: 0 us -> 7.37 us
  between operations: 20.3 us -> 13.1 us
    another operation x33 -> x0, other arithmetic: 256 us -> none  [the longest x30 173 us: body(): factor = jnp.linalg.cholesky(gram)]
    psum x1 -> x0, waiting for transfers between devices: 149 us -> none  [body(): gram = lax.psum(cross(gathered, gathered), 'pair')]
    pallas_call x0 -> x1, Pallas kernels: none -> 69.3 us  [solve(): pl.pallas_call(functools.partial(solve_kernel, cols), out_shape=jax.Shape...]
    reduce_scatter x1, waiting for transfers between devices: 0.03 us -> 64.6 us  [body(): lax.psum_scatter(cross(grid_values, point_values), 'pair', scatter_dimens...]
    reduce_scatter x0 -> x1, waiting for transfers between devices: none -> 59.1 us  [body(): lax.psum_scatter(cross(gathered, point_values), 'pair', scatter_dimension...]
    all_gather x0 -> x1, waiting for transfers between devices: none -> 56.4 us  [body(): gram_parts = lax.all_gather(gram, ('pair', 'col'), axis=0, tiled=False)]
    another operation x44 -> x0, matrix products: 43.6 us -> none  [the longest x14 23.1 us: body(): factor = jnp.linalg.cholesky(gram)]
    another operation x37 -> x0, local copies, waits for them, and re-layouts: 25.2 us -> none
  transfers between devices with their start and end apart: 4 -> 4, of which waited for: 3 -> 4; matrix products, arithmetic and copies ran while one was open for 3% -> 1% of each run, Pallas kernels for 0% -> 0%
where the time goes in v1:
time: 349 us; the launch traced here: 348 us
  waiting for transfers between devices  245 us (70%)
  Pallas kernels  69.3 us (20%)
  between operations  13.1 us (4%)
  matrix products  11.7 us (3%)
  blocking collectives  7.37 us (2%)
    pallas_call x1, Pallas kernels, solve(): pl.pallas_call(functools.partial(solve_kernel, cols), out_shape=jax.Shape...  69.3 us
    reduce_scatter x1, waiting for transfers between devices, body(): lax.psum_scatter(cross(grid_values, point_values), 'pair', scatter_dimens...  64.6 us
    all_gather x1, waiting for transfers between devices, body(): gathered = lax.all_gather(point_values, 'col', axis=1, tiled=True)  63.7 us
    reduce_scatter x1, waiting for transfers between devices, body(): lax.psum_scatter(cross(gathered, point_values), 'pair', scatter_dimension...  59.1 us
    all_gather x1, waiting for transfers between devices, body(): gram_parts = lax.all_gather(gram, ('pair', 'col'), axis=0, tiled=False)  56.4 us
    dot_general x2, matrix products, cross(): lax.dot_general(left, right, (((0,), (0,)), ((), ())), preferred_element_...  11.7 us
    all_to_all x1, blocking collectives, body(): lax.all_to_all(summed, 'col', split_axis=0, concat_axis=1, tiled=True)  7.37 us
  transfers between devices with their start and end apart: 4, of which 4 were waited for; matrix products, arithmetic and copies ran while one was open for 1% of the time, Pallas kernels for 0%

profile of v1, /device:TPU:0, one launch (start us, length us, event | category | flops | bytes accessed | tf_op | source)
XLA Modules:
  0.0 348.4 jit_solution(2314771390687277883)
XLA Ops:
  6.5 0.0 all-gather.4.cloned.1.call-start
  6.5 0.7 all-gather.4.cloned.1.call-update
  7.3 0.0 copy-start.1
  7.3 0.0 reduce-scatter.3.cloned.1.call-start
  7.3 63.7 %all-gather.4.cloned.1.call-done = bf16[4096,1024]{1,0:T(8,128)(2,1)} async-done(((bf16[4096,256]{1,0:T(8,128)(2,1)}), bf16[4096,1024]{1,0:T(8,128)(2,1)}) %all-gather.4.cloned.1.call-update) | async-done | bytes 8388624 | tf_op jit(solution)/shard_map/all_gather | solution.py:117
  71.0 7.4 %fusion = f32[1024,256]{1,0:T(8,128)} fusion(bf16[4096,1024]{1,0:T(8,128)(2,1)} %all-gather.4.cloned.1.call-done, bf16[4096,256]{1,0:T(8,128)(2,1)} %param.2), kind=kOutput, calls=%fused_computation | convolution fusion | flops 2147483648 | bytes 11534336 | tf_op jit(solution)/shard_map/dot_general | solution.py:16
  78.4 0.0 reduce-scatter.3.cloned.1.call-update
  78.5 0.0 reduce-scatter.5.cloned.1.call-start
  78.5 0.0 copy-done.1
  78.5 4.3 %fusion.1 = f32[512,256]{1,0:T(8,128)} fusion(bf16[4096,512]{1,0:T(8,128)(2,1)} %param.3, bf16[4096,256]{1,0:T(8,128)(2,1)S(1)} %copy-done.1), kind=kOutput, calls=%fused_computation.1 | convolution fusion | flops 1073741824 | bytes 6815744 | tf_op jit(solution)/shard_map/dot_general | solution.py:16
  82.8 0.0 reduce-scatter.5.cloned.1.call-update
  82.8 0.0 all-gather.6.cloned.1.call-start
  82.9 59.1 %reduce-scatter.3.cloned.1.call-done = f32[128,256]{1,0:T(8,128)} async-done(((f32[1024,256]{1,0:T(8,128)}), f32[128,256]{1,0:T(8,128)}) %reduce-scatter.3.cloned.1.call-update) | async-done | bytes 131088 | tf_op jit(solution)/shard_map/reduce_scatter | solution.py:118
  141.9 0.0 all-gather.6.cloned.1.call-update
  142.0 64.6 %reduce-scatter.5.cloned.1.call-done = f32[64,256]{1,0:T(8,128)} async-done(((f32[512,256]{1,0:T(8,128)}), f32[64,256]{1,0:T(8,128)}) %reduce-scatter.5.cloned.1.call-update) | async-done | bytes 65552 | tf_op jit(solution)/shard_map/reduce_scatter | solution.py:122
  206.6 7.4 %all_to_all.19 = f32[4,16,256]{2,1,0:T(8,128)S(1)} all-to-all(f32[4,16,256]{2,1,0:T(8,128)} %bitcast.12), channel_id=1, replica_groups=mesh['pair'=8,'col'=4] {'col'}, dimensions={0} | all-to-all | bytes 131072 | tf_op jit(solution)/shard_map/all_to_all | solution.py:125
  214.0 56.4 %all-gather.6.cloned.1.call-done = f32[4096,256]{1,0:T(8,128)} async-done(((f32[128,256]{1,0:T(8,128)}), f32[4096,256]{1,0:T(8,128)}) %all-gather.6.cloned.1.call-update) | async-done | bytes 4194320 | tf_op jit(solution)/shard_map/all_gather | solution.py:121
  270.4 0.0 copy-start
  270.4 2.2 copy-done
  272.6 69.3 %shard_map.28 = f32[16,1024]{1,0:T(8,128)} custom-call(f32[32,128,256]{2,1,0:T(8,128)S(1)} %bitcast.9, f32[16,1024]{1,0:T(8,128)S(1)} %bitcast.10), custom_call_target="tpu_custom_call" | custom-call | tf_op jit(solution)/shard_map/pallas_call | solution.py:100
  (1 shorter events, 0.0 us)
Async XLA Ops:
  6.5 64.5 %all-gather.4.cloned.1.call-start = ((), (), s32[]{:S(2)}) async-start(), calls=%async_computation.3 | async-start | bytes 10485760 | tf_op jit(solution)/shard_map/all_gather | solution.py:117
  7.3 71.3 %copy-start.1 = (bf16[4096,256]{1,0:T(8,128)(2,1)S(1)}, bf16[4096,256]{1,0:T(8,128)(2,1)}, u32[]{:S(2)}) copy-start(bf16[4096,256]{1,0:T(8,128)(2,1)} %param.2) | copy-start | bytes 6291460
  7.3 134.7 %reduce-scatter.3.cloned.1.call-start = ((), (), s32[]{:S(2)}) async-start(), calls=%async_computation.4 | async-start | bytes 1179648 | tf_op jit(solution)/shard_map/reduce_scatter | solution.py:118
  78.5 128.1 %reduce-scatter.5.cloned.1.call-start = ((), (), s32[]{:S(2)}) async-start(), calls=%async_computation.5 | async-start | bytes 589824 | tf_op jit(solution)/shard_map/reduce_scatter | solution.py:122
  82.8 187.6 %all-gather.6.cloned.1.call-start = ((), (), s32[]{:S(2)}) async-start(), calls=%async_computation.6 | async-start | bytes 4325376 | tf_op jit(solution)/shard_map/all_gather | solution.py:121
  270.4 2.2 copy-start
Sparse Core Ops, SparseCore 0:
  8.9 62.0 all-gather.3
  78.6 63.3 reduce-scatter.2
  145.7 60.9 reduce-scatter.4
  209.3 61.0 all-gather.5

commit v2 on v1

--- a/solution.py
+++ b/solution.py
@@ -54,15 +54,31 @@
     return tiles
 
 
-def solve_kernel(cols, gram_ref, rhs_ref, out_ref, work, inverse):
+def solve_kernel(cols, folded, gram_ref, rhs_ref, out_ref, work, inverse):
     n = work.shape[1]
     rows = rhs_ref.shape[0]
     blocks = n // NB
     width = n // cols
+    height = gram_ref.shape[1]
     for i in range(gram_ref.shape[0]):
         p, c = divmod(i, cols)
-        height = gram_ref.shape[1]
-        work[p * height : (p + 1) * height, c * width : (c + 1) * width] = gram_ref[i]
+        part, at = divmod(p * height, width)
+        if not folded or part < 2:
+            block = c ^ part if folded else part
+            top = block * width + at
+            work[top : top + height, c * width : (c + 1) * width] = gram_ref[i]
+    if folded:
+        def part_of(part, c):
+            first = part * width // height
+            return jnp.concatenate(
+                [gram_ref[(first + h) * cols + c] for h in range(width // height)], axis=0
+            )
+        for part in (2, 3):
+            for c in range(2):
+                row, col = c ^ 2, c ^ (part - 2)
+                total = part_of(part, c) + part_of(part, c ^ part).T
+                work[row * width : (row + 1) * width, col * width : (col + 1) * width] = total
+                work[col * width : (col + 1) * width, row * width : (row + 1) * width] = total.T
     work[n : n + rows, :] = rhs_ref[...]
 
     def step(k, carry):
@@ -94,11 +110,11 @@
         out_ref[:, lo:hi] = x
 
 
-def solve(gram_parts, rhs, cols):
+def solve(gram_parts, rhs, cols, folded):
     rows, n = rhs.shape
     vmem = pl.BlockSpec(memory_space=pltpu.VMEM)
     return pl.pallas_call(
-        functools.partial(solve_kernel, cols),
+        functools.partial(solve_kernel, cols, folded),
         out_shape=jax.ShapeDtypeStruct((rows, n), jnp.float32),
         in_specs=[vmem, vmem],
         out_specs=vmem,
@@ -110,20 +126,41 @@
     )(gram_parts, rhs)
 
 
+def fold(own):
+    c = lax.axis_index("col")
+    half = own.shape[0] // 2
+    y = c // 2
+    other = lax.dynamic_slice_in_dim(own, (1 - y) * half, half, 0)
+    received = lax.ppermute(other, "col", [(i, i ^ 2) for i in range(4)])
+    sibling = lax.ppermute(own, "col", [(i, i ^ 1) for i in range(4)])
+    own_half = lax.dynamic_slice_in_dim(own, y * half, half, 0)
+    sibling_half = lax.dynamic_slice_in_dim(sibling, y * half, half, 0)
+    return jnp.concatenate(
+        [cross(own, own), cross(sibling, own), cross(received, own_half), cross(received, sibling_half)],
+        axis=0,
+    )
+
+
 def solution(mesh):
-    cols = mesh.shape["col"]
+    cols, pairs = mesh.shape["col"], mesh.shape["pair"]
+    folded = cols == 4
 
     def body(point_values, grid_values):
-        gathered = lax.all_gather(point_values, "col", axis=1, tiled=True)
-        gram = lax.psum_scatter(
-            cross(gathered, point_values), "pair", scatter_dimension=0, tiled=True
+        project = cross(grid_values, point_values)
+        if folded:
+            gram = fold(point_values)
+        else:
+            gathered = lax.all_gather(point_values, "col", axis=1, tiled=True)
+            gram = cross(gathered, point_values)
+        width = gram.shape[1]
+        both = jnp.concatenate(
+            [gram.reshape(pairs, -1, width), project.reshape(pairs, -1, width)], axis=1
         )
-        gram_parts = lax.all_gather(gram, ("pair", "col"), axis=0, tiled=False)
-        summed = lax.psum_scatter(
-            cross(grid_values, point_values), "pair", scatter_dimension=0, tiled=True
-        )
-        regrouped = lax.all_to_all(summed, "col", split_axis=0, concat_axis=1, tiled=True)
-        return solve(gram_parts, regrouped, cols)
+        own = lax.psum_scatter(both, "pair", scatter_dimension=0, tiled=False)
+        height = gram.shape[0] // pairs
+        gram_parts = lax.all_gather(own[:height], ("pair", "col"), axis=0, tiled=False)
+        regrouped = lax.all_to_all(own[height:], "col", split_axis=0, concat_axis=1, tiled=True)
+        return solve(gram_parts, regrouped, cols, folded)
 
     in_specs = (P("pair", "col"), P("pair", None))
     out_specs = P(("pair", "col"), None)

time: 349 us -> 252 us (0.72)
  waiting for transfers between devices: 245 us -> 142 us
  local copies, waits for them, and re-layouts: 2.2 us -> 8.5 us
  matrix products: 11.7 us -> 6.53 us
    all_gather x2 -> x1, waiting for transfers between devices: 120 us -> 55.1 us  [body(): lax.all_gather(own[:height], ('pair', 'col'), axis=0, tiled=False)]
    reduce_scatter x2 -> x1, waiting for transfers between devices: 124 us -> 66.4 us  [body(): own = lax.psum_scatter(both, 'pair', scatter_dimension=0, tiled=False)]
    ppermute x0 -> x2, waiting for transfers between devices: none -> 20.4 us  [the longest x1 20.4 us: fold(): received = lax.ppermute(other, 'col', [(i, i ^ 2) for i in range(4)])]
    dot_general x2 -> x5, matrix products: 11.7 us -> 6.53 us  [cross(): lax.dot_general(left, right, (((0,), (0,)), ((), ())), preferred_element_...]
  transfers between devices with their start and end apart: 4 -> 4, of which waited for: 4 -> 3; matrix products, arithmetic and copies ran while one was open for 1% -> 2% of each run, Pallas kernels for 0% -> 0%
where the time goes in v2:
time: 252 us; the launch traced here: 251 us
  waiting for transfers between devices  142 us (56%)
  Pallas kernels  69.7 us (28%)
  between operations  13.5 us (5%)
  local copies, waits for them, and re-layouts  8.5 us (3%)
  blocking collectives  6.62 us (3%)
  matrix products  6.53 us (3%)
  starting transfers between devices  3 us (1%)
    pallas_call x1, Pallas kernels, solve(): pl.pallas_call(functools.partial(solve_kernel, cols, folded), out_shape=j...  69.7 us
    reduce_scatter x1, waiting for transfers between devices, body(): own = lax.psum_scatter(both, 'pair', scatter_dimension=0, tiled=False)  66.4 us
    all_gather x1, waiting for transfers between devices, body(): lax.all_gather(own[:height], ('pair', 'col'), axis=0, tiled=False)  55.1 us
    ppermute x1, waiting for transfers between devices, fold(): received = lax.ppermute(other, 'col', [(i, i ^ 2) for i in range(4)])  20.4 us
    all_to_all x1, blocking collectives, body(): lax.all_to_all(own[height:], 'col', split_axis=0, concat_axis=1, tiled=True)  6.62 us
    dot_general x5, matrix products, cross(): lax.dot_general(left, right, (((0,), (0,)), ((), ())), preferred_element_...  6.53 us
  transfers between devices with their start and end apart: 4, of which 3 were waited for; matrix products, arithmetic and copies ran while one was open for 2% of the time, Pallas kernels for 0%

profile of v2, /device:TPU:0, one launch (start us, length us, event | category | flops | bytes accessed | tf_op | source)
XLA Modules:
  0.0 251.2 jit_solution(18050269313254243064)
XLA Ops:
  6.5 0.0 reduce-scatter.2.cloned.1.call-start
  6.5 0.5 collective-permute-start
  7.0 2.4 constant_dynamic-slice_fusion
  9.4 2.5 collective-permute-start.1
  12.0 0.7 fusion.6
  12.7 1.4 copy-done.2
  14.1 1.3 fusion.8
  15.4 20.4 %collective-permute-done.1 = bf16[2048,256]{1,0:T(8,128)(2,1)S(1)} collective-permute-done((bf16[2048,256]{1,0:T(8,128)(2,1)}, bf16[2048,256]{1,0:T(8,128)(2,1)S(1)}, u32[]{:S(2)}, u32[]{:S(2)}) %collective-permute-start.1) | collective-permute-done | bytes 1048608 | tf_op jit(solution)/shard_map/ppermute | solution.py:134
  35.8 0.5 fusion.2
  36.3 0.0 collective-permute-done
  36.3 1.7 fusion
  38.0 2.3 fusion.7
  40.4 0.1 pad_maximum_fusion.1
  40.4 1.3 pad_maximum_fusion
  41.7 0.0 reduce-scatter.2.cloned.1.call-update
  41.7 0.0 all-gather.2.cloned.1.call-start
  41.8 66.4 %reduce-scatter.2.cloned.1.call-done = f32[1,192,256]{2,1,0:T(8,128)} async-done(((f32[8,192,256]{2,1,0:T(8,128)}), f32[1,192,256]{2,1,0:T(8,128)}) %reduce-scatter.2.cloned.1.call-update) | async-done | bytes 196624 | tf_op jit(solution)/shard_map/reduce_scatter | solution.py:159
  108.2 1.6 slice.10
  109.8 0.0 all-gather.2.cloned.1.call-update
  109.8 0.8 slice.11
  110.6 6.6 %all_to_all.19 = f32[4,16,256]{2,1,0:T(8,128)S(1)} all-to-all(f32[4,16,256]{2,1,0:T(8,128)S(1)} %bitcast.17), channel_id=1, replica_groups=mesh['pair'=8,'col'=4] {'col'}, dimensions={0} | all-to-all | bytes 131072 | tf_op jit(solution)/shard_map/all_to_all | solution.py:162
  117.3 55.1 %all-gather.2.cloned.1.call-done.gram_ref = f32[32,128,256]{2,1,0:T(8,128)} async-done(((f32[1,128,256]{2,1,0:T(8,128)}), f32[32,128,256]{2,1,0:T(8,128)}) %all-gather.2.cloned.1.call-update) | async-done | bytes 4194320 | tf_op jit(solution)/shard_map/all_gather | solution.py:161
  172.4 2.2 copy-done
  174.6 69.7 %shard_map.28 = f32[16,1024]{1,0:T(8,128)} custom-call(f32[32,128,256]{2,1,0:T(8,128)S(1)} %copy-done, f32[16,1024]{1,0:T(8,128)S(1)} %bitcast.14), custom_call_target="tpu_custom_call" | custom-call | tf_op jit(solution)/shard_map/pallas_call | solution.py:116
  (5 shorter events, 0.0 us)
Async XLA Ops:
  6.5 5.4 %copy-start.1 = (bf16[4096,256]{1,0:T(8,128)(2,1)S(1)}, bf16[4096,256]{1,0:T(8,128)(2,1)}, u32[]{:S(2)}) copy-start(bf16[4096,256]{1,0:T(8,128)(2,1)} %param.2) | copy-start | bytes 6291460
  6.5 101.7 %reduce-scatter.2.cloned.1.call-start = ((), (), s32[]{:S(2)}) async-start(), calls=%async_computation.2 | async-start | bytes 1769472 | tf_op jit(solution)/shard_map/reduce_scatter | solution.py:159
  6.5 29.8 %collective-permute-start = (bf16[4096,256]{1,0:T(8,128)(2,1)}, bf16[4096,256]{1,0:T(8,128)(2,1)}, u32[]{:S(2)}, u32[]{:S(2)}) collective-permute-start(bf16[4096,256]{1,0:T(8,128)(2,1)} %param.2), channel_id=1, source_target_pairs={{0,1},{1,0},{2,3},{3,2},{4,5},{5,4},{6,7},{7,6},{8,9},{9,8},{10,11... | collective-permute-start | bytes 6291464 | tf_op jit(solution)/shard_map/ppermute | solution.py:135
  9.4 26.4 %collective-permute-start.1 = (bf16[2048,256]{1,0:T(8,128)(2,1)}, bf16[2048,256]{1,0:T(8,128)(2,1)S(1)}, u32[]{:S(2)}, u32[]{:S(2)}) collective-permute-start(bf16[2048,256]{1,0:T(8,128)(2,1)} %constant_dynamic-slice_fusion), channel_id=1, source_target_pairs={{0,2},{1,3},{2,0},{3,1},{4,6},{5,7},{6,4},{7,5},{8,10},{9,11},{10,... | collective-permute-start | bytes 3145736 | tf_op jit(solution)/shard_map/ppermute | solution.py:134
  12.0 2.2 copy-start.2
  41.7 130.7 %all-gather.2.cloned.1.call-start = ((), (), s32[]{:S(2)}) async-start(), calls=%async_computation.3 | async-start | bytes 4325376 | tf_op jit(solution)/shard_map/all_gather | solution.py:161
  172.4 2.2 copy-start
Sparse Core Ops, SparseCore 0:
  41.8 66.3 reduce-scatter.1
  111.5 60.8 all-gather.1

commit v3 on v2

--- a/solution.py
+++ b/solution.py
@@ -156,7 +156,8 @@
         both = jnp.concatenate(
             [gram.reshape(pairs, -1, width), project.reshape(pairs, -1, width)], axis=1
         )
-        own = lax.psum_scatter(both, "pair", scatter_dimension=0, tiled=False)
+        exchanged = lax.all_to_all(both, "pair", split_axis=0, concat_axis=0, tiled=True)
+        own = jnp.sum(exchanged, axis=0)
         height = gram.shape[0] // pairs
         gram_parts = lax.all_gather(own[:height], ("pair", "col"), axis=0, tiled=False)
         regrouped = lax.all_to_all(own[height:], "col", split_axis=0, concat_axis=1, tiled=True)

time: 252 us -> 224 us (0.89)
  waiting for transfers between devices: 142 us -> 74.9 us
  blocking collectives: 6.62 us -> 49.3 us
    reduce_scatter x1 -> x0, waiting for transfers between devices: 66.4 us -> none  [body(): own = lax.psum_scatter(both, 'pair', scatter_dimension=0, tiled=False)]
    all_to_all x0 -> x1, blocking collectives: none -> 42.6 us  [body(): lax.all_to_all(both, 'pair', split_axis=0, concat_axis=0, tiled=True)]
  transfers between devices with their start and end apart: 4 -> 3, of which waited for: 3 -> 2; matrix products, arithmetic and copies ran while one was open for 2% -> 2% of each run, Pallas kernels for 0% -> 0%
where the time goes in v3:
time: 224 us
  waiting for transfers between devices  74.9 us (33%)
  Pallas kernels  69.7 us (31%)
  blocking collectives  49.3 us (22%)
  between operations  13.5 us (6%)
  local copies, waits for them, and re-layouts  6.74 us (3%)
  matrix products  6.53 us (3%)
  starting transfers between devices  2.96 us (1%)
    pallas_call x1, Pallas kernels, solve(): pl.pallas_call(functools.partial(solve_kernel, cols, folded), out_shape=j...  69.7 us
    all_gather x1, waiting for transfers between devices, body(): lax.all_gather(own[:height], ('pair', 'col'), axis=0, tiled=False)  54.5 us
    all_to_all x1, blocking collectives, body(): lax.all_to_all(both, 'pair', split_axis=0, concat_axis=0, tiled=True)  42.6 us
    ppermute x1, waiting for transfers between devices, fold(): received = lax.ppermute(other, 'col', [(i, i ^ 2) for i in range(4)])  20.4 us
    all_to_all x1, blocking collectives, body(): lax.all_to_all(own[height:], 'col', split_axis=0, concat_axis=1, tiled=True)  6.72 us
    dot_general x5, matrix products, cross(): lax.dot_general(left, right, (((0,), (0,)), ((), ())), preferred_element_...  6.53 us
  transfers between devices with their start and end apart: 3, of which 2 were waited for; matrix products, arithmetic and copies ran while one was open for 2% of the time, Pallas kernels for 0%

profile of v3, /device:TPU:0, one launch (start us, length us, event | category | flops | bytes accessed | tf_op | source)
XLA Modules:
  0.0 223.9 jit_solution(11738797357072980641)
XLA Ops:
  6.5 0.0 copy-start.1
  6.5 0.0 all-gather.3.cloned.1.call-start
  6.5 0.5 collective-permute-start
  7.0 2.5 %constant_dynamic-slice_fusion = bf16[2048,256]{1,0:T(8,128)(2,1)} fusion(bf16[4096,256]{1,0:T(8,128)(2,1)} %param.2, s32[]{:T(128)S(6)} %select_n.13), kind=kLoop, calls=%fused_computation.8 | loop fusion | bytes 2097156 | tf_op jit(solution)/shard_map/dynamic_slice | solution.py:133
  9.4 2.5 %collective-permute-start.1 = (bf16[2048,256]{1,0:T(8,128)(2,1)}, bf16[2048,256]{1,0:T(8,128)(2,1)S(1)}, u32[]{:S(2)}, u32[]{:S(2)}) collective-permute-start(bf16[2048,256]{1,0:T(8,128)(2,1)} %constant_dynamic-slice_fusion), channel_id=1, source_target_pairs={{0,2},{1,3},{2,0},{3,1},{4,6},{5,7},{6,4},{7,5},{8,10},{9,11},{10,... | collective-permute-start | bytes 3145736 | tf_op jit(solution)/shard_map/ppermute | solution.py:134
  12.0 0.0 copy-done.1
  12.0 0.7 fusion.6
  12.7 1.4 copy-done.2
  14.1 1.3 fusion.8
  15.4 20.4 %collective-permute-done.1 = bf16[2048,256]{1,0:T(8,128)(2,1)S(1)} collective-permute-done((bf16[2048,256]{1,0:T(8,128)(2,1)}, bf16[2048,256]{1,0:T(8,128)(2,1)S(1)}, u32[]{:S(2)}, u32[]{:S(2)}) %collective-permute-start.1) | collective-permute-done | bytes 1048608 | tf_op jit(solution)/shard_map/ppermute | solution.py:134
  35.8 0.5 fusion.2
  36.3 0.0 collective-permute-done
  36.3 1.7 fusion
  38.0 2.3 %fusion.7 = f32[256,256]{1,0:T(8,128)S(1)} fusion(bf16[4096,256]{1,0:T(8,128)(2,1)} %collective-permute-done, bf16[4096,256]{1,0:T(8,128)(2,1)S(1)} %copy-done.1), kind=kOutput, calls=%fused_computation.10 | convolution fusion | flops 536870912 | bytes 4456448 | tf_op jit(solution)/shard_map/dot_general | solution.py:16
  40.4 0.1 pad_maximum_fusion.1
  40.4 0.1 pad_maximum_fusion
  40.6 42.6 %all_to_all.24 = f32[8,192,256]{2,1,0:T(8,128)S(1)} all-to-all(f32[8,192,256]{2,1,0:T(8,128)S(1)} %pad_maximum_fusion), channel_id=1, replica_groups=mesh['pair'=8,'col'=4] {'pair'}, dimensions={0} | all-to-all | bytes 3145728 | tf_op jit(solution)/shard_map/all_to_all | solution.py:159
  83.1 0.1 reduce_sum.9
  83.2 0.6 slice.8
  83.9 0.0 all-gather.3.cloned.1.call-update
  83.9 6.7 %all_to_all.25 = f32[4,16,256]{2,1,0:T(8,128)S(1)} all-to-all(f32[4,16,256]{2,1,0:T(8,128)S(1)} %bitcast.19), channel_id=1, replica_groups=mesh['pair'=8,'col'=4] {'col'}, dimensions={0} | all-to-all | bytes 131072 | tf_op jit(solution)/shard_map/all_to_all | solution.py:163
  90.7 54.5 %all-gather.3.cloned.1.call-done = f32[4096,256]{1,0:T(8,128)} async-done(((f32[128,256]{1,0:T(8,128)}), f32[4096,256]{1,0:T(8,128)}) %all-gather.3.cloned.1.call-update) | async-done | bytes 4194320 | tf_op jit(solution)/shard_map/all_gather | solution.py:162
  145.1 2.2 copy-done
  147.3 69.7 %shard_map.28 = f32[16,1024]{1,0:T(8,128)} custom-call(f32[32,128,256]{2,1,0:T(8,128)S(1)} %bitcast.15, f32[16,1024]{1,0:T(8,128)S(1)} %bitcast.16), custom_call_target="tpu_custom_call" | custom-call | tf_op jit(solution)/shard_map/pallas_call | solution.py:116
  (4 shorter events, 0.0 us)
Async XLA Ops:
  6.5 5.4 %copy-start.1 = (bf16[4096,256]{1,0:T(8,128)(2,1)S(1)}, bf16[4096,256]{1,0:T(8,128)(2,1)}, u32[]{:S(2)}) copy-start(bf16[4096,256]{1,0:T(8,128)(2,1)} %param.2) | copy-start | bytes 6291460
  6.5 138.6 %all-gather.3.cloned.1.call-start = ((), (), s32[]{:S(2)}) async-start(), calls=%async_computation.2 | async-start | bytes 4325376 | tf_op jit(solution)/shard_map/all_gather | solution.py:162
  6.5 29.8 %collective-permute-start = (bf16[4096,256]{1,0:T(8,128)(2,1)}, bf16[4096,256]{1,0:T(8,128)(2,1)}, u32[]{:S(2)}, u32[]{:S(2)}) collective-permute-start(bf16[4096,256]{1,0:T(8,128)(2,1)} %param.2), channel_id=1, source_target_pairs={{0,1},{1,0},{2,3},{3,2},{4,5},{5,4},{6,7},{7,6},{8,9},{9,8},{10,11... | collective-permute-start | bytes 6291464 | tf_op jit(solution)/shard_map/ppermute | solution.py:135
  9.4 26.4 %collective-permute-start.1 = (bf16[2048,256]{1,0:T(8,128)(2,1)}, bf16[2048,256]{1,0:T(8,128)(2,1)S(1)}, u32[]{:S(2)}, u32[]{:S(2)}) collective-permute-start(bf16[2048,256]{1,0:T(8,128)(2,1)} %constant_dynamic-slice_fusion), channel_id=1, source_target_pairs={{0,2},{1,3},{2,0},{3,1},{4,6},{5,7},{6,4},{7,5},{8,10},{9,11},{10,... | collective-permute-start | bytes 3145736 | tf_op jit(solution)/shard_map/ppermute | solution.py:134
  12.0 2.2 copy-start.2
  145.1 2.2 copy-start
Sparse Core Ops, SparseCore 0:
  84.0 61.0 all-gather.2

commit v4 on v3

--- a/solution.py
+++ b/solution.py
@@ -60,25 +60,45 @@
     blocks = n // NB
     width = n // cols
     height = gram_ref.shape[1]
-    for i in range(gram_ref.shape[0]):
-        p, c = divmod(i, cols)
-        part, at = divmod(p * height, width)
-        if not folded or part < 2:
-            block = c ^ part if folded else part
-            top = block * width + at
-            work[top : top + height, c * width : (c + 1) * width] = gram_ref[i]
     if folded:
-        def part_of(part, c):
-            first = part * width // height
-            return jnp.concatenate(
-                [gram_ref[(first + h) * cols + c] for h in range(width // height)], axis=0
+        half = width // 2
+        quarter = half // 2
+
+        def put(row, col, block):
+            h, w = block.shape
+            work[row : row + h, col : col + w] = block
+
+        held = []
+        for c in range(cols):
+            held.append(jnp.concatenate(
+                [gram_ref[p * cols + c] for p in range(gram_ref.shape[0] // cols)], axis=0
+            ))
+        cross_at = half + quarter + half
+        for c in range(cols):
+            at = c * width
+            low = held[c][:half]
+            corner = held[c][half : half + quarter]
+            put(at + half, at, low)
+            put(at, at + half, low[:, :half].T)
+            put(at, at, corner[:, :half])
+            put(at + quarter, at, corner[:, half:])
+        for c in (0, 2):
+            both = jnp.concatenate(
+                [held[c + core][half + quarter : cross_at] for core in range(2)], axis=0
             )
+            put(c * width, (c + 1) * width, both)
+            put((c + 1) * width, c * width, both.T)
         for part in (2, 3):
+            first = cross_at + (part - 2) * width
             for c in range(2):
                 row, col = c ^ 2, c ^ (part - 2)
-                total = part_of(part, c) + part_of(part, c ^ part).T
-                work[row * width : (row + 1) * width, col * width : (col + 1) * width] = total
-                work[col * width : (col + 1) * width, row * width : (row + 1) * width] = total.T
+                total = held[c][first : first + width] + held[c ^ part][first : first + width].T
+                put(row * width, col * width, total)
+                put(col * width, row * width, total.T)
+    else:
+        for i in range(gram_ref.shape[0]):
+            p, c = divmod(i, cols)
+            work[p * height : (p + 1) * height, c * width : (c + 1) * width] = gram_ref[i]
     work[n : n + rows, :] = rhs_ref[...]
 
     def step(k, carry):
@@ -135,15 +155,22 @@
     sibling = lax.ppermute(own, "col", [(i, i ^ 1) for i in range(4)])
     own_half = lax.dynamic_slice_in_dim(own, y * half, half, 0)
     sibling_half = lax.dynamic_slice_in_dim(sibling, y * half, half, 0)
+    square = cross(own, own)
+    width = square.shape[0]
+    mid = width // 2
+    corner = square[:mid, :mid]
+    corner = jnp.concatenate([corner[: mid // 2], corner[mid // 2 :]], axis=1)
+    beside = cross(sibling, own)
+    beside = jnp.where(c % 2 == 0, beside.T[:mid], beside[mid:])
     return jnp.concatenate(
-        [cross(own, own), cross(sibling, own), cross(received, own_half), cross(received, sibling_half)],
+        [square[mid:], corner, beside, cross(received, own_half), cross(received, sibling_half)],
         axis=0,
     )
 
 
 def solution(mesh):
     cols, pairs = mesh.shape["col"], mesh.shape["pair"]
-    folded = cols == 4
+    folded = cols == 4 and pairs == 8
 
     def body(point_values, grid_values):
         project = cross(grid_values, point_values)

time: 224 us -> 218 us (0.973)
  waiting for transfers between devices: 74.9 us -> 66.4 us
  blocking collectives: 49.3 us -> 45.7 us
  other arithmetic: 0.28 us -> 3.53 us
    ppermute x1, waiting for transfers between devices: 20.4 us -> 14.8 us  [fold(): received = lax.ppermute(other, 'col', [(i, i ^ 2) for i in range(4)])]
    all_to_all x1, blocking collectives: 42.6 us -> 39 us  [body(): lax.all_to_all(both, 'pair', split_axis=0, concat_axis=0, tiled=True)]
    all_gather x1, waiting for transfers between devices: 54.5 us -> 51.6 us  [body(): lax.all_gather(own[:height], ('pair', 'col'), axis=0, tiled=False)]
  transfers between devices with their start and end apart: 3 -> 3, of which waited for: 2 -> 2; matrix products, arithmetic and copies ran while one was open for 2% -> 5% of each run, Pallas kernels for 0% -> 0%
where the time goes in v4:
time: 218 us; the launch traced here: 217 us
  Pallas kernels  69.9 us (32%)
  waiting for transfers between devices  66.4 us (30%)
  blocking collectives  45.7 us (21%)
  between operations  13.4 us (6%)
  matrix products  8.74 us (4%)
  local copies, waits for them, and re-layouts  6.77 us (3%)
  other arithmetic  3.53 us (2%)
  starting transfers between devices  2.96 us (1%)
    pallas_call x1, Pallas kernels, solve(): pl.pallas_call(functools.partial(solve_kernel, cols, folded), out_shape=j...  69.9 us
    all_gather x1, waiting for transfers between devices, body(): lax.all_gather(own[:height], ('pair', 'col'), axis=0, tiled=False)  51.6 us
    all_to_all x1, blocking collectives, body(): lax.all_to_all(both, 'pair', split_axis=0, concat_axis=0, tiled=True)  39 us
    ppermute x1, waiting for transfers between devices, fold(): received = lax.ppermute(other, 'col', [(i, i ^ 2) for i in range(4)])  14.8 us
    dot_general x5, matrix products, cross(): lax.dot_general(left, right, (((0,), (0,)), ((), ())), preferred_element_...  8.74 us
    all_to_all x1, blocking collectives, body(): lax.all_to_all(own[height:], 'col', split_axis=0, concat_axis=1, tiled=True)  6.71 us
  transfers between devices with their start and end apart: 3, of which 2 were waited for; matrix products, arithmetic and copies ran while one was open for 5% of the time, Pallas kernels for 0%

profile of v4, /device:TPU:0, one launch (start us, length us, event | category | flops | bytes accessed | tf_op | source)
XLA Modules:
  0.0 217.4 jit_solution(719898854162009711)
XLA Ops:
  6.5 0.5 collective-permute-start
  7.0 2.5 %constant_dynamic-slice_fusion = bf16[2048,256]{1,0:T(8,128)(2,1)} fusion(bf16[4096,256]{1,0:T(8,128)(2,1)} %param.2, s32[]{:T(128)S(6)} %select_n.30), kind=kLoop, calls=%fused_computation.11 | loop fusion | bytes 2097156 | tf_op jit(solution)/shard_map/dynamic_slice | solution.py:153
  9.4 2.5 %collective-permute-start.1 = (bf16[2048,256]{1,0:T(8,128)(2,1)}, bf16[2048,256]{1,0:T(8,128)(2,1)S(1)}, u32[]{:S(2)}, u32[]{:S(2)}) collective-permute-start(bf16[2048,256]{1,0:T(8,128)(2,1)} %constant_dynamic-slice_fusion), channel_id=1, source_target_pairs={{0,2},{1,3},{2,0},{3,1},{4,6},{5,7},{6,4},{7,5},{8,10},{9,11},{10,... | collective-permute-start | bytes 3145736 | tf_op jit(solution)/shard_map/ppermute | solution.py:154
  12.0 0.7 fusion.6
  12.7 0.7 slice_dynamic-update-slice_fusion
  13.4 0.6 maximum_dynamic-update-slice_fusion
  14.0 0.2 copy-done.3
  14.2 2.1 fusion.8
  16.3 0.0 collective-permute-done
  16.3 2.3 %fusion.7 = f32[256,256]{1,0:T(8,128)S(1)} fusion(bf16[4096,256]{1,0:T(8,128)(2,1)} %collective-permute-done, bf16[4096,256]{1,0:T(8,128)(2,1)S(1)} %copy-done.1), kind=kOutput, calls=%fused_computation.14 | convolution fusion | flops 536870912 | bytes 4456448 | tf_op jit(solution)/shard_map/dot_general | solution.py:16
  18.6 0.8 copy.4
  19.4 1.6 fusion.2
  21.0 14.8 %collective-permute-done.1 = bf16[2048,256]{1,0:T(8,128)(2,1)S(1)} collective-permute-done((bf16[2048,256]{1,0:T(8,128)(2,1)}, bf16[2048,256]{1,0:T(8,128)(2,1)S(1)}, u32[]{:S(2)}, u32[]{:S(2)}) %collective-permute-start.1) | collective-permute-done | bytes 1048608 | tf_op jit(solution)/shard_map/ppermute | solution.py:154
  35.8 1.2 convolution_dynamic-update-slice_fusion.1
  37.0 2.4 %convolution_dynamic-update-slice_fusion = f32[832,256]{1,0:T(8,128)} fusion(f32[832,256]{1,0:T(8,128)} %convolution_dynamic-update-slice_fusion.1, bf16[2048,256]{1,0:T(8,128)(2,1)S(1)} %collective-permute-done.1, bf16[4096,256]{1,0:T(8,128)(2,1)} %collective-permute-done, s32[]{:T(128)S(6)} %select_n.31), kind=kOutput, calls=%fused_computation.1 | convolution fusion | flops 268435456 | bytes 2359300 | tf_op jit(solution)/shard_map/dot_general | solution.py:16
  39.4 1.2 pad_maximum_fusion
  40.7 39.0 %all_to_all.24 = f32[8,168,256]{2,1,0:T(8,128)S(1)} all-to-all(f32[8,168,256]{2,1,0:T(8,128)S(1)} %pad_maximum_fusion), channel_id=1, replica_groups=mesh['pair'=8,'col'=4] {'pair'}, dimensions={0} | all-to-all | bytes 2752512 | tf_op jit(solution)/shard_map/all_to_all | solution.py:186
  79.6 0.1 reduce_sum.9
  79.7 0.6 slice.36
  80.4 0.0 all-gather.3.cloned.1.call-update
  80.4 6.7 %all_to_all.25 = f32[4,16,256]{2,1,0:T(8,128)S(1)} all-to-all(f32[4,16,256]{2,1,0:T(8,128)S(1)} %bitcast.20), channel_id=1, replica_groups=mesh['pair'=8,'col'=4] {'col'}, dimensions={0} | all-to-all | bytes 131072 | tf_op jit(solution)/shard_map/all_to_all | solution.py:190
  87.1 51.6 %all-gather.3.cloned.1.call-done = f32[3328,256]{1,0:T(8,128)} async-done(((f32[104,256]{1,0:T(8,128)}), f32[3328,256]{1,0:T(8,128)}) %all-gather.3.cloned.1.call-update) | async-done | bytes 3407888 | tf_op jit(solution)/shard_map/all_gather | solution.py:189
  138.7 2.0 copy-done
  140.7 69.9 %shard_map.28 = f32[16,1024]{1,0:T(8,128)} custom-call(f32[32,104,256]{2,1,0:T(8,128)S(1)} %bitcast.16, f32[16,1024]{1,0:T(8,128)S(1)} %bitcast.17), custom_call_target="tpu_custom_call" | custom-call | tf_op jit(solution)/shard_map/pallas_call | solution.py:136
  (10 shorter events, 0.0 us)
Async XLA Ops:
  6.5 5.4 %copy-start.1 = (bf16[4096,256]{1,0:T(8,128)(2,1)S(1)}, bf16[4096,256]{1,0:T(8,128)(2,1)}, u32[]{:S(2)}) copy-start(bf16[4096,256]{1,0:T(8,128)(2,1)} %param.2) | copy-start | bytes 6291460
  6.5 132.2 %all-gather.3.cloned.1.call-start = ((), (), s32[]{:S(2)}) async-start(), calls=%async_computation.2 | async-start | bytes 3514368 | tf_op jit(solution)/shard_map/all_gather | solution.py:189
  6.5 9.7 %collective-permute-start = (bf16[4096,256]{1,0:T(8,128)(2,1)}, bf16[4096,256]{1,0:T(8,128)(2,1)}, u32[]{:S(2)}, u32[]{:S(2)}) collective-permute-start(bf16[4096,256]{1,0:T(8,128)(2,1)} %param.2), channel_id=1, source_target_pairs={{0,1},{1,0},{2,3},{3,2},{4,5},{5,4},{6,7},{7,6},{8,9},{9,8},{10,11... | collective-permute-start | bytes 6291464 | tf_op jit(solution)/shard_map/ppermute | solution.py:155
  9.4 26.4 %collective-permute-start.1 = (bf16[2048,256]{1,0:T(8,128)(2,1)}, bf16[2048,256]{1,0:T(8,128)(2,1)S(1)}, u32[]{:S(2)}, u32[]{:S(2)}) collective-permute-start(bf16[2048,256]{1,0:T(8,128)(2,1)} %constant_dynamic-slice_fusion), channel_id=1, source_target_pairs={{0,2},{1,3},{2,0},{3,1},{4,6},{5,7},{6,4},{7,5},{8,10},{9,11},{10,... | collective-permute-start | bytes 3145736 | tf_op jit(solution)/shard_map/ppermute | solution.py:154
  12.0 2.2 %copy-start.3 = (bf16[4096,512]{1,0:T(8,128)(2,1)S(1)}, bf16[4096,512]{1,0:T(8,128)(2,1)}, u32[]{:S(2)}) copy-start(bf16[4096,512]{1,0:T(8,128)(2,1)} %param.3) | copy-start | bytes 12582916
  21.0 18.4 %copy-start.2 = (f32[512,256]{1,0:T(8,128)S(1)}, f32[512,256]{1,0:T(8,128)}, u32[]{:S(2)}) copy-start(f32[512,256]{1,0:T(8,128)} %fusion.8) | copy-start | bytes 1572868
  138.7 2.0 copy-start
Sparse Core Ops, SparseCore 0:
  80.5 58.1 all-gather.2
